TPU v7x, 256 devices: a whole 4x4x8 slice. The times are simulated.
256 devices in a mesh: pp: 8 (over y, core), ep: 32 (over x, z).
Axes of the slice: x: 4, y: 4, z: 8, core: 2. Of those that a mesh axis runs over, the one named last changes fastest.
Arguments:
- fwd_in: bfloat16 [8, 4096, 3584], P('pp', 'ep'), may hold values from -6 to 6
- fwd_ids: int32 [8, 4096, 1], P('pp', 'ep'), may hold values from 0 to 7; in each aligned block of 128 rows (0 to 127, 128 to 255, ..., all dimensions but the last counted through in order) at most 20 rows name the same one
- saved_in: bfloat16 [8, 4096, 3584], P('pp', 'ep'), may hold values from -6 to 6
- bwd_ids: int32 [8, 4096, 1], P('pp', 'ep'), may hold values from 0 to 7; in each aligned block of 128 rows (0 to 127, 128 to 255, ..., all dimensions but the last counted through in order) at most 20 rows name the same one
- grad_in: bfloat16 [8, 4096, 3584], P('pp', 'ep'), may hold values from -6 to 6
- router: float32 [8, 3584, 8], P('pp'), may hold values from -0.09375 to 0.09375
- w_gate: bfloat16 [8, 3584, 8192], P('pp', None, 'ep'), may hold values from -0.09375 to 0.09375
- w_up: bfloat16 [8, 3584, 8192], P('pp', None, 'ep'), may hold values from -0.09375 to 0.09375
- w_down: bfloat16 [8, 8192, 3584], P('pp', 'ep'), may hold values from -0.1875 to 0.1875
Outputs:
- fwd_next: bfloat16 [8, 4096, 3584], P('pp', 'ep')
- grad_next: bfloat16 [8, 4096, 3584], P('pp', 'ep')
Inputs may be any that keep to these rules, and one draw needn't show every extreme that they name: `fwd_ids`: within the 128 tokens of one device's aligned block, no expert is chosen more than 20 times; some block chooses some expert exactly 20 times. `bwd_ids`: as for fwd_ids.
All inputs are finite; a program needn't handle non-finite values.
Results may differ from a plain program's by a relative error of at most 0.011.
Values may be sent and summed in bfloat16 or wider, within the bound.
A program may use at most 128 MiB of HBM per device.

v0:
```python
import jax
import jax.numpy as jnp
from jax import lax
from jax.sharding import PartitionSpec as P

route_scale = 2.5
contract = (((1,), (1,)), ((), ()))


def swapped(value, axis, distance):
    return lax.ppermute(value, axis, [(i, i ^ 1 << distance) for i in range(lax.axis_size(axis))])


def from_behind(value, axis, steps):
    count = lax.axis_size(axis)
    pairs = [(source, (source + steps) % count) for source in range(count)]
    return lax.ppermute(value, axis, pairs)


def order_slots(chosen, experts, capacity):
    token_count = chosen.shape[0]
    onehot = (chosen[:, None] == jnp.arange(experts, dtype=jnp.int32)[None, :]).astype(jnp.int32)
    before = jnp.cumsum(onehot, axis=0) - onehot
    ranking = jnp.sum(before * onehot, axis=1)
    slot_table = jnp.full((experts * capacity,), token_count, jnp.int32)
    slot_table = slot_table.at[chosen * capacity + ranking].set(
        jnp.arange(token_count, dtype=jnp.int32)
    )
    return (onehot, ranking, slot_table)


def routing_weight(tokens, router, onehot):
    logits = jnp.dot(tokens.astype(jnp.float32), router, precision=lax.Precision.HIGHEST)
    picked = jnp.sum(jnp.where(onehot > 0, logits, 0.0), axis=1)
    return route_scale * jax.nn.sigmoid(picked)


def with_zero_row(tokens):
    return jnp.concatenate([tokens, jnp.zeros((1, tokens.shape[1]), tokens.dtype)], axis=0)


def expert_forward(row_block, gate_cols, up_cols, down_rows):
    gate_proj = jnp.dot(row_block, gate_cols, preferred_element_type=jnp.float32)
    up_proj = jnp.dot(row_block, up_cols, preferred_element_type=jnp.float32)
    hidden = (gate_proj * jax.nn.sigmoid(gate_proj) * up_proj).astype(jnp.bfloat16)
    return jnp.dot(hidden, down_rows, preferred_element_type=jnp.float32).astype(jnp.bfloat16)


def expert_backward(row_block, row_grads, joined_cols, down_rows):
    unit_count = down_rows.shape[0]
    both_proj = jnp.dot(row_block, joined_cols, preferred_element_type=jnp.float32)
    gate_proj = both_proj[:, :unit_count]
    up_proj = both_proj[:, unit_count:]
    d_hidden = lax.dot_general(row_grads, down_rows, contract, preferred_element_type=jnp.float32)
    sigmoid_gate = jax.nn.sigmoid(gate_proj)
    d_gate = (d_hidden * up_proj * sigmoid_gate * (1.0 + gate_proj * (1.0 - sigmoid_gate))).astype(
        jnp.bfloat16
    )
    d_up = (d_hidden * gate_proj * sigmoid_gate).astype(jnp.bfloat16)
    d_joined = jnp.concatenate([d_gate, d_up], axis=1)
    partial_sum = lax.dot_general(
        d_joined, joined_cols, contract, preferred_element_type=jnp.float32
    )
    return partial_sum.astype(jnp.bfloat16)


def arrange(own_rows, peer_rows, own_bit):
    return jnp.where(
        own_bit == 0, jnp.stack([own_rows, peer_rows]), jnp.stack([peer_rows, own_rows])
    )


def per_device(fwd_in, fwd_ids, saved_in, bwd_ids, grad_in, router, w_gate, w_up, w_down):
    experts = router.shape[-1]
    owners = lax.axis_size("ep")
    group_size = owners // experts
    bit_count = group_size.bit_length() - 1
    own_index = lax.axis_index("ep")
    token_count = fwd_in.shape[1]
    width = fwd_in.shape[2]
    capacity = group_size * max(1, 5 * token_count // (4 * experts * group_size))
    quarter_slots = capacity // group_size
    router_section = router[0]
    gate_cols = w_gate[0]
    up_cols = w_up[0]
    down_rows = w_down[0]
    joined_cols = jnp.concatenate([gate_cols, up_cols], axis=1)
    fwd_tokens = fwd_in[0]
    fwd_chosen = fwd_ids[0, :, 0]
    fwd_onehot, fwd_rank, fwd_table = order_slots(fwd_chosen, experts, capacity)
    fwd_weight = routing_weight(fwd_tokens, router_section, fwd_onehot)
    fwd_padded = with_zero_row(fwd_tokens)
    saved_tokens = saved_in[0]
    bwd_chosen = bwd_ids[0, :, 0]
    grad_tokens = grad_in[0]
    bwd_onehot, bwd_rank, bwd_table = order_slots(bwd_chosen, experts, capacity)
    bwd_weight = routing_weight(saved_tokens, router_section, bwd_onehot)
    weighted = (bwd_weight[:, None] * grad_tokens.astype(jnp.float32)).astype(jnp.bfloat16)
    saved_padded = with_zero_row(saved_tokens)
    weighted_padded = with_zero_row(weighted)
    fwd_index = (
        fwd_table.reshape(experts, quarter_slots, group_size)
        .transpose(0, 2, 1)
        .reshape(owners, quarter_slots)
    )
    gathered = lax.all_to_all(
        jnp.take(fwd_padded, fwd_index, axis=0), "ep", split_axis=0, concat_axis=0, tiled=True
    )
    for bit_number in range(bit_count):
        own_bit = own_index >> bit_number & 1
        peer_rows = swapped(gathered, "ep", bit_number)
        gathered = arrange(gathered, peer_rows, own_bit)
    partial_out = expert_forward(gathered.reshape(-1, width), gate_cols, up_cols, down_rows)
    partial_out = partial_out.reshape(group_size, 1, owners * quarter_slots, width)
    for bit_number in reversed(range(bit_count)):
        own_bit = own_index >> bit_number & 1
        half_rows = partial_out.shape[0] // 2
        kept_half = lax.dynamic_slice_in_dim(partial_out, own_bit * half_rows, half_rows, 0)
        sent_half = lax.dynamic_slice_in_dim(partial_out, (1 - own_bit) * half_rows, half_rows, 0)
        partial_out = jnp.concatenate([kept_half, swapped(sent_half, "ep", bit_number)], axis=1)
    summed = jnp.sum(partial_out, axis=(0, 1), dtype=jnp.float32).astype(jnp.bfloat16)
    returned = lax.all_to_all(
        summed.reshape(owners, quarter_slots, width), "ep", split_axis=0, concat_axis=0, tiled=True
    ).reshape(-1, width)
    source_slot = (
        fwd_chosen * group_size + fwd_rank % group_size
    ) * quarter_slots + fwd_rank // group_size
    fwd_expert = jnp.take(returned, source_slot, axis=0).astype(jnp.float32)
    bwd_index = (
        bwd_table.reshape(experts, quarter_slots, group_size)
        .transpose(0, 2, 1)
        .reshape(owners, quarter_slots)
    )
    saved_rows, grad_rows = (
        lax.all_to_all(
            jnp.take(saved_padded, bwd_index, axis=0), "ep", split_axis=0, concat_axis=0, tiled=True
        ),
        lax.all_to_all(
            jnp.take(weighted_padded, bwd_index, axis=0),
            "ep",
            split_axis=0,
            concat_axis=0,
            tiled=True,
        ),
    )
    for bit_number in range(bit_count):
        own_bit = own_index >> bit_number & 1
        peer_saved, peer_grads = swapped((saved_rows, grad_rows), "ep", bit_number)
        saved_rows = arrange(saved_rows, peer_saved, own_bit)
        grad_rows = arrange(grad_rows, peer_grads, own_bit)
    partial_grad = expert_backward(
        saved_rows.reshape(-1, width), grad_rows.reshape(-1, width), joined_cols, down_rows
    )
    partial_grad = partial_grad.reshape(group_size, 1, owners * quarter_slots, width)
    for bit_number in reversed(range(bit_count)):
        own_bit = own_index >> bit_number & 1
        half_rows = partial_grad.shape[0] // 2
        kept_half = lax.dynamic_slice_in_dim(partial_grad, own_bit * half_rows, half_rows, 0)
        sent_half = lax.dynamic_slice_in_dim(partial_grad, (1 - own_bit) * half_rows, half_rows, 0)
        partial_grad = jnp.concatenate([kept_half, swapped(sent_half, "ep", bit_number)], axis=1)
    summed_grad = jnp.sum(partial_grad, axis=(0, 1), dtype=jnp.float32).astype(jnp.bfloat16)
    returned_grad = lax.all_to_all(
        summed_grad.reshape(owners, quarter_slots, width),
        "ep",
        split_axis=0,
        concat_axis=0,
        tiled=True,
    ).reshape(-1, width)
    grad_slot = (
        bwd_chosen * group_size + bwd_rank % group_size
    ) * quarter_slots + bwd_rank // group_size
    bwd_expert = jnp.take(returned_grad, grad_slot, axis=0).astype(jnp.float32)
    fwd_section = (fwd_tokens.astype(jnp.float32) + fwd_weight[:, None] * fwd_expert).astype(
        jnp.bfloat16
    )
    grad_section = (grad_tokens.astype(jnp.float32) + bwd_expert).astype(jnp.bfloat16)
    fwd_next = from_behind(fwd_section[None], "pp", 1)
    grad_next = from_behind(grad_section[None], "pp", -1)
    return (fwd_next, grad_next)


def solution(mesh):
    in_specs = (
        P("pp", "ep", None),
        P("pp", "ep", None),
        P("pp", "ep", None),
        P("pp", "ep", None),
        P("pp", "ep", None),
        P("pp", None, None),
        P("pp", None, "ep"),
        P("pp", None, "ep"),
        P("pp", "ep", None),
    )
    out_specs = (P("pp", "ep", None), P("pp", "ep", None))
    return jax.shard_map(
        per_device, mesh=mesh, in_specs=in_specs, out_specs=out_specs, check_vma=False
    )
```

profile of v0, /device:TPU:1, one launch (start us, length us, event | category | flops | bytes accessed | tf_op | source)
XLA Modules:
  0.0 915.1 jit_solution(13571112951853104166)
XLA Ops:
  25.3 53.2 %all_to_all.25 = bf16[32,5,3584]{2,1,0:T(8,128)(2,1)} all-to-all(bf16[32,5,3584]{2,1,0:T(8,128)(2,1)S(1)} %get-tuple-element.24), channel_id=1, replica_groups=mesh['pp'=8,'ep'=32] {'ep'}, dimensions={0} | all-to-all | bytes 2293760 | tf_op jit(solution)/shard_map/all_to_all | solution.py:135
  78.5 8.8 all-to-all-start.2
  96.8 33.5 %all-to-all-done.2 = bf16[32,5,3584]{2,1,0:T(8,128)(2,1)} async-done(((bf16[32,5,3584]{2,1,0:T(8,128)(2,1)}), bf16[32,5,3584]{2,1,0:T(8,128)(2,1)}, u32[]{:S(2)}, u32[]{:S(2)}) %all-to-all-start.2) | async-done | bytes 1146912 | tf_op jit(solution)/shard_map/all_to_all | solution.py:138
  130.3 7.2 all-to-all-start
  144.9 35.8 %all-to-all-done = bf16[32,5,3584]{2,1,0:T(8,128)(2,1)} async-done(((bf16[32,5,3584]{2,1,0:T(8,128)(2,1)}), bf16[32,5,3584]{2,1,0:T(8,128)(2,1)}, u32[]{:S(2)}, u32[]{:S(2)}) %all-to-all-start) | async-done | bytes 1146912 | tf_op jit(solution)/shard_map/all_to_all | solution.py:106
  184.8 18.2 %collective-permute-done.7 = bf16[32,5,3584]{2,0,1:T(8,128)(2,1)} collective-permute-done((bf16[32,5,3584]{2,0,1:T(8,128)(2,1)}, bf16[32,5,3584]{2,0,1:T(8,128)(2,1)}, u32[]{:S(2)}, u32[]{:S(2)}) %collective-permute-start.7) | collective-permute-done | bytes 1146912 | tf_op jit(solution)/shard_map/ppermute | solution.py:11
  208.1 64.0 %collective-permute-done.5 = bf16[32,5,3584]{2,0,1:T(8,128)(2,1)} collective-permute-done((bf16[32,5,3584]{2,0,1:T(8,128)(2,1)}, bf16[32,5,3584]{2,0,1:T(8,128)(2,1)}, u32[]{:S(2)}, u32[]{:S(2)}) %collective-permute-start.5) | collective-permute-done | bytes 1146912 | tf_op jit(solution)/shard_map/ppermute | solution.py:11
  278.3 18.4 %collective-permute-done = bf16[32,5,3584]{2,0,1:T(8,128)(2,1)S(1)} collective-permute-done((bf16[32,5,3584]{2,0,1:T(8,128)(2,1)}, bf16[32,5,3584]{2,0,1:T(8,128)(2,1)S(1)}, u32[]{:S(2)}, u32[]{:S(2)}) %collective-permute-start) | collective-permute-done | bytes 1146912 | tf_op jit(solution)/shard_map/ppermute | solution.py:11
  307.3 4.6 maximum_select_fusion.3
  311.8 91.9 %collective-permute-done.8 = bf16[2,32,5,3584]{3,1,2,0:T(8,128)(2,1)S(1)} collective-permute-done((bf16[2,32,5,3584]{3,1,2,0:T(8,128)(2,1)S(1)}, bf16[2,32,5,3584]{3,1,2,0:T(8,128)(2,1)S(1)}, u32[]{:S(2)}, u32[]{:S(2)}) %collective-permute-start.8) | collective-permute-done | bytes 2293792 | tf_op jit(solution)/shard_map/ppermute | solution.py:11
  409.0 43.9 %collective-permute-done.6 = bf16[2,32,5,3584]{3,1,2,0:T(8,128)(2,1)S(1)} collective-permute-done((bf16[2,32,5,3584]{3,1,2,0:T(8,128)(2,1)S(1)}, bf16[2,32,5,3584]{3,1,2,0:T(8,128)(2,1)S(1)}, u32[]{:S(2)}, u32[]{:S(2)}) %collective-permute-start.6) | collective-permute-done | bytes 2293792 | tf_op jit(solution)/shard_map/ppermute | solution.py:11
  454.2 4.0 maximum_select_fusion.1
  458.2 8.1 select_n.188
  466.3 8.1 select_n.184
  474.4 6.1 fusion
  488.1 63.2 %collective-permute-done.1 = bf16[2,32,5,3584]{3,1,2,0:T(8,128)(2,1)} collective-permute-done((bf16[2,32,5,3584]{3,1,2,0:T(8,128)(2,1)}, bf16[2,32,5,3584]{3,1,2,0:T(8,128)(2,1)}, u32[]{:S(2)}, u32[]{:S(2)}) %collective-permute-start.1) | collective-permute-done | bytes 2293792 | tf_op jit(solution)/shard_map/ppermute | solution.py:11
  554.2 4.0 maximum_select_fusion
  558.3 8.1 select_n.172
  566.4 4.2 fusion.42
  570.6 9.8 %convolution_convert_fusion.1 = bf16[640,3584]{1,0:T(8,128)(2,1)} fusion(bf16[1,256,3584]{2,1,0:T(8,128)(2,1)S(1)} %copy-done, f32[640,256]{1,0:T(8,128)S(1)} %fusion.42, bf16[640,3584]{1,0:T(8,128)(2,1)} %select_n.172, bf16[1,3584,256]{2,1,0:T(8,128)(2,1)} %param.20), kind=kOutput, calls=%fused_computation.11 | convolution fusion | flops 2352087040 | bytes 13500416 | tf_op jit(solution)/shard_map/dot_general | solution.py:46
  580.5 4.8 constant_dynamic-slice_fusion.2
  585.2 64.4 %collective-permute-done.9 = bf16[2,1,160,3584]{3,2,0,1:T(8,128)(2,1)} collective-permute-done((bf16[2,1,160,3584]{3,2,0,1:T(8,128)(2,1)}, bf16[2,1,160,3584]{3,2,0,1:T(8,128)(2,1)}, u32[]{:S(2)}, u32[]{:S(2)}) %collective-permute-start.9) | collective-permute-done | bytes 2293792 | tf_op jit(solution)/shard_map/ppermute | solution.py:11
  649.6 5.5 fusion.1
  656.3 42.5 %collective-permute-done.2 = bf16[2,1,160,3584]{3,2,0,1:T(8,128)(2,1)} collective-permute-done((bf16[2,1,160,3584]{3,2,0,1:T(8,128)(2,1)}, bf16[2,1,160,3584]{3,2,0,1:T(8,128)(2,1)}, u32[]{:S(2)}, u32[]{:S(2)}) %collective-permute-start.2) | collective-permute-done | bytes 2293792 | tf_op jit(solution)/shard_map/ppermute | solution.py:11
  698.8 5.9 fusion.4
  706.1 45.0 %collective-permute-done.10 = bf16[1,2,160,3584]{3,2,0,1:T(8,128)(2,1)} collective-permute-done((bf16[1,2,160,3584]{3,2,0,1:T(8,128)(2,1)S(1)}, bf16[1,2,160,3584]{3,2,0,1:T(8,128)(2,1)}, u32[]{:S(2)}, u32[]{:S(2)}) %collective-permute-start.10) | collective-permute-done | bytes 2293792 | tf_op jit(solution)/shard_map/ppermute | solution.py:11
  758.4 8.8 all-to-all-start.4
  767.1 52.8 %collective-permute-done.3 = bf16[1,2,160,3584]{3,2,0,1:T(8,128)(2,1)} collective-permute-done((bf16[1,2,160,3584]{3,2,0,1:T(8,128)(2,1)}, bf16[1,2,160,3584]{3,2,0,1:T(8,128)(2,1)}, u32[]{:S(2)}, u32[]{:S(2)}) %collective-permute-start.3) | collective-permute-done | bytes 2293792 | tf_op jit(solution)/shard_map/ppermute | solution.py:11
  827.1 13.4 %all-to-all-done.4 = bf16[32,5,3584]{2,1,0:T(8,128)(2,1)} async-done(((bf16[32,5,3584]{2,1,0:T(8,128)(2,1)}), bf16[32,5,3584]{2,1,0:T(8,128)(2,1)}, u32[]{:S(2)}, u32[]{:S(2)}) %all-to-all-start.4) | async-done | bytes 1146912 | tf_op jit(solution)/shard_map/all_to_all | solution.py:162
  840.6 8.5 all-to-all-start.1
  857.3 34.9 %all-to-all-done.1 = bf16[32,5,3584]{2,1,0:T(8,128)(2,1)} async-done(((bf16[32,5,3584]{2,1,0:T(8,128)(2,1)}), bf16[32,5,3584]{2,1,0:T(8,128)(2,1)}, u32[]{:S(2)}, u32[]{:S(2)}) %all-to-all-start.1) | async-done | bytes 1146912 | tf_op jit(solution)/shard_map/all_to_all | solution.py:122
  901.5 10.3 %collective-permute-done.4 = bf16[1,128,3584]{2,1,0:T(8,128)(2,1)S(1)} collective-permute-done((bf16[1,128,3584]{2,1,0:T(8,128)(2,1)S(1)}, bf16[1,128,3584]{2,1,0:T(8,128)(2,1)S(1)}, u32[]{:S(2)}, u32[]{:S(2)}) %collective-permute-start.4) | collective-permute-done | bytes 917536 | tf_op jit(solution)/shard_map/ppermute | solution.py:17
  (124 shorter events, 122.0 us)
Async XLA Ops:
  0.6 479.9 %copy-start = (bf16[1,256,3584]{2,1,0:T(8,128)(2,1)S(1)}, bf16[1,256,3584]{2,1,0:T(8,128)(2,1)}, u32[]{:S(2)}) copy-start(bf16[1,256,3584]{2,1,0:T(8,128)(2,1)} %param.21) | copy-start | bytes 5505028
  0.6 9.5 %copy-start.6 = (bf16[1,128,3584]{2,1,0:T(8,128)(2,1)S(1)}, bf16[1,128,3584]{2,1,0:T(8,128)(2,1)}, u32[]{:S(2)}) copy-start(bf16[1,128,3584]{2,1,0:T(8,128)(2,1)} %param.17) | copy-start | bytes 2752516
  78.5 51.8 %all-to-all-start.2 = ((bf16[32,5,3584]{2,1,0:T(8,128)(2,1)}), bf16[32,5,3584]{2,1,0:T(8,128)(2,1)}, u32[]{:S(2)}, u32[]{:S(2)}) async-start(bf16[32,5,3584]{2,1,0:T(8,128)(2,1)} %get-tuple-element.25), calls=%async_computation.2 | async-start | bytes 3670016 | tf_op jit(solution)/shard_map/all_to_all | solution.py:138
  130.3 50.3 %all-to-all-start = ((bf16[32,5,3584]{2,1,0:T(8,128)(2,1)}), bf16[32,5,3584]{2,1,0:T(8,128)(2,1)}, u32[]{:S(2)}, u32[]{:S(2)}) async-start(bf16[32,5,3584]{2,1,0:T(8,128)(2,1)} %broadcast_select_fusion.2), calls=%async_computation | async-start | bytes 3670016 | tf_op jit(solution)/shard_map/all_to_all | solution.py:106
  140.4 62.5 %collective-permute-start.7 = (bf16[32,5,3584]{2,0,1:T(8,128)(2,1)}, bf16[32,5,3584]{2,0,1:T(8,128)(2,1)}, u32[]{:S(2)}, u32[]{:S(2)}) collective-permute-start(bf16[32,5,3584]{2,0,1:T(8,128)(2,1)} %copy.65), channel_id=1, source_target_pairs={{0,1},{1,0},{2,3},{3,2},{4,5},{5,4},{6,7},{7,6},{8,9},{9,8},{10,11... | collective-permute-start | bytes 3440648 | tf_op jit(solution)/shard_map/ppermute | solution.py:11
  144.6 127.6 %collective-permute-start.5 = (bf16[32,5,3584]{2,0,1:T(8,128)(2,1)}, bf16[32,5,3584]{2,0,1:T(8,128)(2,1)}, u32[]{:S(2)}, u32[]{:S(2)}) collective-permute-start(bf16[32,5,3584]{2,0,1:T(8,128)(2,1)} %copy.58), channel_id=1, source_target_pairs={{0,1},{1,0},{2,3},{3,2},{4,5},{5,4},{6,7},{7,6},{8,9},{9,8},{10,11... | collective-permute-start | bytes 3440648 | tf_op jit(solution)/shard_map/ppermute | solution.py:11
  183.6 113.0 %collective-permute-start = (bf16[32,5,3584]{2,0,1:T(8,128)(2,1)}, bf16[32,5,3584]{2,0,1:T(8,128)(2,1)S(1)}, u32[]{:S(2)}, u32[]{:S(2)}) collective-permute-start(bf16[32,5,3584]{2,0,1:T(8,128)(2,1)} %copy.48), channel_id=1, source_target_pairs={{0,1},{1,0},{2,3},{3,2},{4,5},{5,4},{6,7},{7,6},{8,9},{9,8},{10,11... | collective-permute-start | bytes 3440648 | tf_op jit(solution)/shard_map/ppermute | solution.py:11
  184.8 20.1 %copy-start.1 = (bf16[32,5,3584]{2,1,0:T(8,128)(2,1)S(1)}, bf16[32,5,3584]{2,1,0:T(8,128)(2,1)}, u32[]{:S(2)}) copy-start(bf16[32,5,3584]{2,1,0:T(8,128)(2,1)} %all_to_all.25) | copy-start | bytes 3440644
  206.7 197.0 %collective-permute-start.8 = (bf16[2,32,5,3584]{3,1,2,0:T(8,128)(2,1)S(1)}, bf16[2,32,5,3584]{3,1,2,0:T(8,128)(2,1)S(1)}, u32[]{:S(2)}, u32[]{:S(2)}) collective-permute-start(bf16[2,32,5,3584]{3,1,2,0:T(8,128)(2,1)S(1)} %copy.68), channel_id=1, source_target_pairs={{0,2},{1,3},{2,0},{3,1},{4,6},{5,7},{6,4},{7,5},{8,10},{9,11},{10,... | collective-permute-start | bytes 6881288 | tf_op jit(solution)/shard_map/ppermute | solution.py:11
  278.2 174.7 %collective-permute-start.6 = (bf16[2,32,5,3584]{3,1,2,0:T(8,128)(2,1)S(1)}, bf16[2,32,5,3584]{3,1,2,0:T(8,128)(2,1)S(1)}, u32[]{:S(2)}, u32[]{:S(2)}) collective-permute-start(bf16[2,32,5,3584]{3,1,2,0:T(8,128)(2,1)S(1)} %copy.61), channel_id=1, source_target_pairs={{0,2},{1,3},{2,0},{3,1},{4,6},{5,7},{6,4},{7,5},{8,10},{9,11},{10,... | collective-permute-start | bytes 6881288 | tf_op jit(solution)/shard_map/ppermute | solution.py:11
  302.8 248.5 %collective-permute-start.1 = (bf16[2,32,5,3584]{3,1,2,0:T(8,128)(2,1)}, bf16[2,32,5,3584]{3,1,2,0:T(8,128)(2,1)}, u32[]{:S(2)}, u32[]{:S(2)}) collective-permute-start(bf16[2,32,5,3584]{3,1,2,0:T(8,128)(2,1)} %copy.51), channel_id=1, source_target_pairs={{0,2},{1,3},{2,0},{3,1},{4,6},{5,7},{6,4},{7,5},{8,10},{9,11},{10,... | collective-permute-start | bytes 6881288 | tf_op jit(solution)/shard_map/ppermute | solution.py:11
  474.4 6.1 copy-start.5
  480.5 1.5 copy-start.10
  480.6 2.0 copy-start.11
  487.7 66.5 %copy-start.2 = (bf16[1,2,32,5,3584]{4,3,2,1,0:T(8,128)(2,1)S(1)}, bf16[1,2,32,5,3584]{4,3,2,1,0:T(8,128)(2,1)}, u32[]{:S(2)}) copy-start(bf16[1,2,32,5,3584]{4,3,2,1,0:T(8,128)(2,1)} %maximum_select_fusion.3) | copy-start | bytes 6881284
  487.7 161.9 %collective-permute-start.9 = (bf16[2,1,160,3584]{3,2,0,1:T(8,128)(2,1)}, bf16[2,1,160,3584]{3,2,0,1:T(8,128)(2,1)}, u32[]{:S(2)}, u32[]{:S(2)}) collective-permute-start(bf16[2,1,160,3584]{3,2,0,1:T(8,128)(2,1)} %get-tuple-element.10), channel_id=1, source_target_pairs={{0,2},{1,3},{2,0},{3,1},{4,6},{5,7},{6,4},{7,5},{8,10},{9,11},{10,... | collective-permute-start | bytes 6881288 | tf_op jit(solution)/shard_map/ppermute | solution.py:11
  585.2 113.6 %collective-permute-start.2 = (bf16[2,1,160,3584]{3,2,0,1:T(8,128)(2,1)}, bf16[2,1,160,3584]{3,2,0,1:T(8,128)(2,1)}, u32[]{:S(2)}, u32[]{:S(2)}) collective-permute-start(bf16[2,1,160,3584]{3,2,0,1:T(8,128)(2,1)} %get-tuple-element.14), channel_id=1, source_target_pairs={{0,2},{1,3},{2,0},{3,1},{4,6},{5,7},{6,4},{7,5},{8,10},{9,11},{10,... | collective-permute-start | bytes 6881288 | tf_op jit(solution)/shard_map/ppermute | solution.py:11
  649.6 49.2 %copy-start.3 = (bf16[2,1,160,3584]{3,2,0,1:T(8,128)(2,1)S(1)}, bf16[2,1,160,3584]{3,2,0,1:T(8,128)(2,1)}, u32[]{:S(2)}) copy-start(bf16[2,1,160,3584]{3,2,0,1:T(8,128)(2,1)} %get-tuple-element.15) | copy-start | bytes 6881284
  655.1 96.0 %collective-permute-start.10 = (bf16[1,2,160,3584]{3,2,0,1:T(8,128)(2,1)S(1)}, bf16[1,2,160,3584]{3,2,0,1:T(8,128)(2,1)}, u32[]{:S(2)}, u32[]{:S(2)}) collective-permute-start(bf16[1,2,160,3584]{3,2,0,1:T(8,128)(2,1)S(1)} %get-tuple-element.8), channel_id=1, source_target_pairs={{0,1},{1,0},{2,3},{3,2},{4,5},{5,4},{6,7},{7,6},{8,9},{9,8},{10,11... | collective-permute-start | bytes 6881288 | tf_op jit(solution)/shard_map/ppermute | solution.py:11
  704.7 115.3 %collective-permute-start.3 = (bf16[1,2,160,3584]{3,2,0,1:T(8,128)(2,1)}, bf16[1,2,160,3584]{3,2,0,1:T(8,128)(2,1)}, u32[]{:S(2)}, u32[]{:S(2)}) collective-permute-start(bf16[1,2,160,3584]{3,2,0,1:T(8,128)(2,1)} %get-tuple-element.12), channel_id=1, source_target_pairs={{0,1},{1,0},{2,3},{3,2},{4,5},{5,4},{6,7},{7,6},{8,9},{9,8},{10,11... | collective-permute-start | bytes 6881288 | tf_op jit(solution)/shard_map/ppermute | solution.py:11
  758.4 82.2 %all-to-all-start.4 = ((bf16[32,5,3584]{2,1,0:T(8,128)(2,1)}), bf16[32,5,3584]{2,1,0:T(8,128)(2,1)}, u32[]{:S(2)}, u32[]{:S(2)}) async-start(bf16[32,5,3584]{2,1,0:T(8,128)(2,1)} %reduce_sum.101), calls=%async_computation.4 | async-start | bytes 3670016 | tf_op jit(solution)/shard_map/all_to_all | solution.py:162
  827.1 21.9 %copy-start.8 = (s32[1,128,1]{1,2,0:T(1,128)S(1)}, s32[1,128,1]{1,2,0:T(1,128)}, u32[]{:S(2)}) copy-start(s32[1,128,1]{1,2,0:T(1,128)} %param.16) | copy-start | bytes 1540
  827.1 21.9 %copy-start.9 = (s32[1,128,1]{1,2,0:T(1,128)S(1)}, s32[1,128,1]{1,2,0:T(1,128)}, u32[]{:S(2)}) copy-start(s32[1,128,1]{1,2,0:T(1,128)} %param.14) | copy-start | bytes 1540
  827.1 22.0 %copy-start.4 = (bf16[1,128,3584]{2,1,0:T(8,128)(2,1)S(1)}, bf16[1,128,3584]{2,1,0:T(8,128)(2,1)}, u32[]{:S(2)}) copy-start(bf16[1,128,3584]{2,1,0:T(8,128)(2,1)} %param.13) | copy-start | bytes 2752516
  827.1 22.0 %copy-start.7 = (f32[1,3584,8]{1,2,0:T(8,128)S(1)}, f32[1,3584,8]{1,2,0:T(8,128)}, u32[]{:S(2)}) copy-start(f32[1,3584,8]{1,2,0:T(8,128)} %param.18) | copy-start | bytes 344068
  840.6 51.5 %all-to-all-start.1 = ((bf16[32,5,3584]{2,1,0:T(8,128)(2,1)}), bf16[32,5,3584]{2,1,0:T(8,128)(2,1)}, u32[]{:S(2)}, u32[]{:S(2)}) async-start(bf16[32,5,3584]{2,1,0:T(8,128)(2,1)} %reduce_sum.94), calls=%async_computation.1 | async-start | bytes 3670016 | tf_op jit(solution)/shard_map/all_to_all | solution.py:122
  856.5 45.0 %collective-permute-start.11 = (bf16[1,128,3584]{2,1,0:T(8,128)(2,1)}, bf16[1,128,3584]{2,1,0:T(8,128)(2,1)}, u32[]{:S(2)}, u32[]{:S(2)}) collective-permute-start(bf16[1,128,3584]{2,1,0:T(8,128)(2,1)} %fusion.15), channel_id=1, source_target_pairs={{0,224},{32,0},{64,32},{96,64},{128,96},{160,128},{192,160},{224,1... | collective-permute-start | bytes 2752520 | tf_op jit(solution)/shard_map/ppermute | solution.py:17
  897.7 14.1 %collective-permute-start.4 = (bf16[1,128,3584]{2,1,0:T(8,128)(2,1)S(1)}, bf16[1,128,3584]{2,1,0:T(8,128)(2,1)S(1)}, u32[]{:S(2)}, u32[]{:S(2)}) collective-permute-start(bf16[1,128,3584]{2,1,0:T(8,128)(2,1)S(1)} %fusion.14), channel_id=1, source_target_pairs={{0,32},{32,64},{64,96},{96,128},{128,160},{160,192},{192,224},{224... | collective-permute-start | bytes 2752520 | tf_op jit(solution)/shard_map/ppermute | solution.py:17
where the time goes:
time: 925 us; the launch traced here: 915 us
  waiting for transfers between devices  632 us (68%)
  local copies, waits for them, and re-layouts  90.8 us (10%)
  other arithmetic  65.5 us (7%)
  blocking collectives  53.2 us (6%)
  starting transfers between devices  45.1 us (5%)
  matrix products  27 us (3%)
    ppermute x10, waiting for transfers between devices, swapped(): lax.ppermute(value, axis, [(i, i ^ 1 << distance) for i in range(lax.axis...  504 us
    all_to_all x1, blocking collectives, per_device(): lax.all_to_all(jnp.take(saved_padded, bwd_index, axis=0), 'ep', split_axi...  53.2 us
    all_to_all x1, waiting for transfers between devices, per_device(): lax.all_to_all(jnp.take(fwd_padded, fwd_index, axis=0), 'ep', split_axis=...  35.8 us
    all_to_all x1, waiting for transfers between devices, per_device(): lax.all_to_all(summed.reshape(owners, quarter_slots, width), 'ep', split_...  34.9 us
    all_to_all x1, waiting for transfers between devices, per_device(): lax.all_to_all(jnp.take(weighted_padded, bwd_index, axis=0), 'ep', split_...  33.5 us
    select_n x9, other arithmetic, arrange(): jnp.where(own_bit == 0, jnp.stack([own_rows, peer_rows]), jnp.stack([peer...  28.4 us
    select_n x6, local copies, waits for them, and re-layouts, arrange(): jnp.where(own_bit == 0, jnp.stack([own_rows, peer_rows]), jnp.stack([peer...  28.1 us
  transfers between devices with their start and end apart: 16, of which 15 were waited for; matrix products, arithmetic and copies ran while one was open for 17% of the time, Pallas kernels for 0%

commit v1 on v0

v1 whole, which is shorter than its diff:
```python
import functools

import jax
import jax.numpy as jnp
from jax import lax
from jax.experimental import pallas as pl
from jax.experimental.pallas import tpu as pltpu
from jax.sharding import PartitionSpec as P

route_scale = 2.5
MESH = pl.DeviceIdType.MESH
f32 = jnp.float32
bf16 = jnp.bfloat16

NX = 4
NZ = 8
SPAN = 4
CAP = 20
MSG = 48
BLK = NX * CAP
OWN = 7
FROM_LEFT, FROM_RIGHT, AWAY = 7, 8, 9
B_AT = 6
B_PREP = 3
LAG = 2
F_DONE = 12
COLS = 512


def nt(a, b):
    return lax.dot_general(a, b, (((1,), (1,)), ((), ())), preferred_element_type=f32)


def nn(a, b):
    return jnp.dot(a, b, preferred_element_type=f32)


def kernel(
    pf, pb, pft, pbt, q, qt, fw, fwd, sav, wgt, grd, wg_h, wu_h, wd_h,
    out_f, out_b,
    tok, wg, wu, wd, xs, xr, inb, away, part, back, ys, yr, sec,
    ld_sem, x_ss, x_rs, in_ss, in_rs, f_ss, o_ss, o_rs, y_ss, y_rs, pp_ss, pp_rs,
):
    width = tok.shape[2]
    chunks = width // COLS
    pp = lax.axis_index("pp")
    ep = lax.axis_index("ep")
    n_pp = lax.axis_size("pp")
    x = ep // NZ
    z = ep % NZ
    h = z // SPAN
    i = z % SPAN

    def at(xx, zz):
        return {"ep": (xx % NX) * NZ + (zz + NZ) % NZ}

    right = at(x, z + 1)
    left = at(x, z - 1)
    pp_up = {"pp": (pp + 1) % n_pp}
    pp_down = {"pp": (pp + n_pp - 1) % n_pp}

    loads = [
        pltpu.make_async_copy(src, dst, ld_sem.at[j])
        for j, (src, dst) in enumerate([
            (fwd, tok.at[0]), (sav, tok.at[1]), (wgt, tok.at[2]), (grd, tok.at[3]),
            (wg_h, wg), (wu_h, wu), (wd_h, wd),
        ])
    ]
    for load in loads:
        load.start()

    barrier = pltpu.get_barrier_semaphore()
    friends = [at(x + 1, z), at(x + 2, z), at(x + 3, z), right, left, at(x, z + 2), at(x, z - 2), pp_up, pp_down]
    for friend in friends:
        pl.semaphore_signal(barrier, inc=1, device_id=friend, device_id_type=MESH)
    pl.semaphore_wait(barrier, len(friends))

    def remote(src, dst, ss, rs, dev):
        return pltpu.make_async_remote_copy(
            src_ref=src, dst_ref=dst, send_sem=ss, recv_sem=rs, device_id=dev, device_id_type=MESH
        )

    def cols(c):
        return pl.ds(pl.multiple_of(c * COLS, COLS), COLS)

    def rows48(k):
        return pl.ds(pl.multiple_of(k * MSG, 16), MSG)

    def x_copy(t, d):
        return remote(xs.at[t, d - 1], xr.at[t, rows48(x), :], x_ss.at[t, d - 1], x_rs.at[t, d - 1], at(x + d, z))

    def x_arrival(t, d):
        return remote(
            xs.at[t, d - 1], xr.at[t, rows48((x + NX - d) % NX), :], x_ss.at[t, d - 1], x_rs.at[t, d - 1], at(x + d, z)
        )

    def x_send(t, p_ref):
        for d in (2, 1, 3, 0):
            xd = (x + d) % NX

            @pl.loop(0, chunks)
            def _(c, d=d, xd=xd):
                picked = nn(p_ref[rows48(xd), :], tok[t, :, cols(c)]).astype(bf16)
                if d == 0:
                    xr[t, rows48(x), cols(c)] = picked
                else:
                    xs[t, d - 1, :, cols(c)] = picked

            if d:
                x_copy(t, d).start()

    def own_right(t):
        return remote(inb.at[t, OWN], inb.at[t, 0], in_ss.at[t, OWN, 0], in_rs.at[t, 0], right)

    def own_left(t):
        return remote(inb.at[t, OWN], inb.at[t, 6], in_ss.at[t, OWN, 1], in_rs.at[t, 6], left)

    def own_away(t):
        slot = jnp.where(i < 2, 6 - i, 3 - i)
        target = at(x, jnp.where(i < 2, z - 1 - i, z + 4 - i))
        return remote(away.at[t], inb.at[t, slot], f_ss.at[t], in_rs.at[t, slot], target)

    def pass_right(t, k):
        return remote(inb.at[t, k - 1], inb.at[t, k], in_ss.at[t, k - 1, 0], in_rs.at[t, k], right)

    def pass_left(t, k):
        return remote(inb.at[t, 7 - k], inb.at[t, 6 - k], in_ss.at[t, 7 - k, 1], in_rs.at[t, 6 - k], left)

    def arrival(t, slot):
        return remote(inb.at[t, slot], inb.at[t, slot], in_ss.at[t, slot, 0], in_rs.at[t, slot], right)

    def has_l(k):
        return (k >= 1) & (k <= i + 2)

    def has_r(k):
        return (k >= 1) & (k <= 5 - i)

    def z_start(t):
        for d in (1, 3, 2):
            x_arrival(t, d).wait_recv()

        @pl.loop(0, chunks)
        def _(c):
            inb[t, OWN, :, cols(c)] = nn(q[h], xr[t, :, cols(c)]).astype(bf16)
            away[t, :, cols(c)] = nn(q[1 - h], xr[t, :, cols(c)]).astype(bf16)

        @pl.when(i < 3)
        def _():
            own_right(t).start()

        @pl.when(i > 0)
        def _():
            own_left(t).start()

        own_away(t).start()

    def z_step(t, k):
        @pl.when(has_l(k))
        def _():
            arrival(t, k - 1).wait_recv()

            @pl.when(i < 3)
            def _():
                pass_right(t, k).start()

        @pl.when(has_r(k))
        def _():
            arrival(t, 7 - k).wait_recv()

            @pl.when(i > 0)
            def _():
                pass_left(t, k).start()

    def expert_forward(slot):
        gate = nn(inb[0, slot], wg[...])
        up = nn(inb[0, slot], wu[...])
        hidden = (gate * jax.nn.sigmoid(gate) * up).astype(bf16)

        @pl.loop(0, chunks)
        def _(c):
            part[0, slot, :, cols(c)] = nn(hidden, wd[:, cols(c)]).astype(bf16)

    def expert_backward(slot):
        gate = nn(inb[1, slot], wg[...])
        up = nn(inb[1, slot], wu[...])
        d_hidden = nt(inb[2, slot], wd[...])
        s = jax.nn.sigmoid(gate)
        d_gate = (d_hidden * up * s * (1.0 + gate * (1.0 - s))).astype(bf16)
        d_up = (d_hidden * gate * s).astype(bf16)

        @pl.loop(0, chunks)
        def _(c):
            part[1, slot, :, cols(c)] = (nt(d_gate, wg[cols(c), :]) + nt(d_up, wu[cols(c), :])).astype(bf16)

    def work(expert, k):
        @pl.loop(0, 2)
        def _(side):
            good = jnp.where(side == 0, has_l(k).astype(jnp.int32), ((k >= 0) & (k <= 5 - i)).astype(jnp.int32))

            @pl.when(good == 1)
            def _():
                expert(jnp.where(side == 0, k - 1, 7 - k))

    def back_left(o, k):
        slot = jnp.where(i == 0, AWAY, jnp.where(k >= 2, k - 2, FROM_RIGHT))
        return remote(
            part.at[o, k - 1], back.at[o, slot], o_ss.at[o, k - 1], o_rs.at[o, slot],
            at(x, jnp.where(i == 0, z - k, z - 1)),
        )

    def back_right(o, k):
        slot = jnp.where(i == 3, AWAY, jnp.where(k >= 2, 8 - k, FROM_LEFT))
        return remote(
            part.at[o, 7 - k], back.at[o, slot], o_ss.at[o, 7 - k], o_rs.at[o, slot],
            at(x, jnp.where(i == 3, z + k, z + 1)),
        )

    def returned(o, slot):
        return remote(back.at[o, slot], back.at[o, slot], o_ss.at[o, 0], o_rs.at[o, slot], right)

    def add_in(o, slot, src):
        returned(o, src).wait_recv()

        @pl.loop(0, chunks)
        def _(c):
            part[o, slot, :, cols(c)] = (
                part[o, slot, :, cols(c)].astype(f32) + back[o, src, :, cols(c)].astype(f32)
            ).astype(bf16)

    def back_step(o, n):
        kl = n - LAG * (3 - i)

        @pl.when(has_l(kl))
        def _():
            @pl.when(i < 3)
            def _():
                add_in(o, kl - 1, kl - 1)

            back_left(o, kl).start()

        kr = n - LAG * i

        @pl.when(has_r(kr))
        def _():
            @pl.when(i > 0)
            def _():
                add_in(o, 7 - kr, 7 - kr)

            back_right(o, kr).start()

    def y_copy(o, d):
        return remote(ys.at[o, d - 1], yr.at[o, rows48(x), :], y_ss.at[o, d - 1], y_rs.at[o, d - 1], at(x + d, z))

    def y_arrival(o, d):
        return remote(
            ys.at[o, d - 1], yr.at[o, rows48((x + NX - d) % NX), :], y_ss.at[o, d - 1], y_rs.at[o, d - 1], at(x + d, z)
        )

    def y_send(o):
        @pl.when(i > 0)
        def _():
            add_in(o, OWN, FROM_LEFT)

        @pl.when(i < 3)
        def _():
            add_in(o, OWN, FROM_RIGHT)

        returned(o, AWAY).wait_recv()
        for d in (2, 1, 3, 0):
            xd = (x + d) % NX

            @pl.loop(0, chunks)
            def _(c, d=d, xd=xd):
                picked = (
                    nn(qt[h, rows48(xd), :], part[o, OWN, :, cols(c)])
                    + nn(qt[1 - h, rows48(xd), :], back[o, AWAY, :, cols(c)])
                ).astype(bf16)
                if d == 0:
                    yr[o, rows48(x), cols(c)] = picked
                else:
                    ys[o, d - 1, :, cols(c)] = picked

            if d:
                y_copy(o, d).start()

    def pp_copy(o):
        if o == 0:
            return remote(sec.at[0], out_f, pp_ss.at[0], pp_rs.at[0], pp_up)
        return remote(sec.at[1], out_b, pp_ss.at[1], pp_rs.at[1], pp_down)

    def finish(o, pt_ref):
        for d in (1, 3, 2):
            y_arrival(o, d).wait_recv()

        @pl.loop(0, chunks)
        def _(c):
            expert_out = nn(pt_ref[...], yr[o, :, cols(c)]).astype(bf16).astype(f32)
            if o == 0:
                sec[o, :, cols(c)] = (tok[0, :, cols(c)].astype(f32) + fw[...] * expert_out).astype(bf16)
            else:
                sec[o, :, cols(c)] = (tok[3, :, cols(c)].astype(f32) + expert_out).astype(bf16)

        pp_copy(o).start()

    loads[0].wait()
    x_send(0, pf)
    loads[1].wait()
    x_send(1, pb)
    loads[2].wait()
    x_send(2, pb)
    z_start(0)
    for j in range(3, 7):
        loads[j].wait()

    last = B_AT + 5 + 3 * LAG

    @pl.loop(0, last + 1)
    def _(n):
        kb = n - B_AT

        @pl.when((n >= 1) & (n <= 5))
        def _():
            z_step(0, n)

        @pl.when(n == B_PREP)
        def _():
            z_start(1)
            z_start(2)

        @pl.when((kb >= 1) & (kb <= 5))
        def _():
            z_step(1, kb)
            z_step(2, kb)

        @pl.when(n <= 5)
        def _():
            work(expert_forward, n)

        @pl.when((kb >= 0) & (kb <= 5))
        def _():
            work(expert_backward, kb)

        back_step(0, n)
        back_step(1, kb)

        @pl.when(n == F_DONE)
        def _():
            y_send(0)

    finish(0, pft)
    y_send(1)
    finish(1, pbt)

    for t in range(3):
        for d in (1, 2, 3):
            x_copy(t, d).wait_send()
        own_away(t).wait_send()

        @pl.when(i < 3)
        def _(t=t):
            own_right(t).wait_send()

        @pl.when(i > 0)
        def _(t=t):
            own_left(t).wait_send()

    @pl.loop(1, 6)
    def _(k):
        for t in range(3):
            @pl.when(has_l(k) & (i < 3))
            def _(t=t):
                pass_right(t, k).wait_send()

            @pl.when(has_r(k) & (i > 0))
            def _(t=t):
                pass_left(t, k).wait_send()

        for o in range(2):
            @pl.when(has_l(k))
            def _(o=o):
                back_left(o, k).wait_send()

            @pl.when(has_r(k))
            def _(o=o):
                back_right(o, k).wait_send()

    for o in range(2):
        for d in (1, 2, 3):
            y_copy(o, d).wait_send()
        pp_copy(o).wait_send()
        pp_copy(o).wait_recv()


def slots(chosen, experts):
    count = chosen.shape[0]
    onehot = (chosen[:, None] == jnp.arange(experts, dtype=jnp.int32)[None, :]).astype(bf16)
    earlier = (jnp.arange(count)[:, None] > jnp.arange(count)[None, :]).astype(bf16)
    before = jnp.dot(earlier, onehot, preferred_element_type=f32)
    rank = jnp.sum(before * onehot.astype(f32), axis=1).astype(jnp.int32)
    place = (chosen // 2) * MSG + (chosen % 2) * CAP + rank
    spots = jnp.arange(NX * MSG, dtype=jnp.int32)
    spread = (spots[:, None] == place[None, :]).astype(bf16)
    gather = (place[:, None] == spots[None, :]).astype(bf16)
    return onehot, spread, gather


def routing_weight(tokens, router, onehot):
    logits = jnp.dot(tokens.astype(f32), router, precision=lax.Precision.HIGHEST)
    picked = jnp.sum(jnp.where(onehot > 0, logits, 0.0), axis=1)
    return route_scale * jax.nn.sigmoid(picked)


def per_device(fwd_in, fwd_ids, saved_in, bwd_ids, grad_in, router, w_gate, w_up, w_down):
    experts = router.shape[-1]
    tokens, width = fwd_in.shape[1:]
    units = w_down.shape[1]
    assert lax.axis_size("ep") == NX * NZ and experts == 2 * NX and tokens == 128
    fwd_hot, pf, pft = slots(fwd_ids[0, :, 0], experts)
    bwd_hot, pb, pbt = slots(bwd_ids[0, :, 0], experts)
    fwd_weight = routing_weight(fwd_in[0], router[0], fwd_hot)
    bwd_weight = routing_weight(saved_in[0], router[0], bwd_hot)
    weighted = (bwd_weight[:, None] * grad_in[0].astype(f32)).astype(bf16)
    block_row = jnp.arange(BLK)
    wide = jnp.arange(NX * MSG)
    source = (block_row // CAP) * MSG + block_row % CAP
    half = jnp.arange(2) * CAP
    q = (source[None, :, None] + half[:, None, None] == wide[None, None, :]).astype(bf16)
    qt = (source[None, None, :] + half[:, None, None] == wide[None, :, None]).astype(bf16)
    shape = jax.ShapeDtypeStruct((tokens, width), bf16)
    vmem = pl.BlockSpec(memory_space=pltpu.VMEM)
    hbm = pl.BlockSpec(memory_space=pl.ANY)
    dma = pltpu.SemaphoreType.DMA
    out_f, out_b = pl.pallas_call(
        kernel,
        out_shape=(shape, shape),
        in_specs=[vmem] * 7 + [hbm] * 7,
        out_specs=(hbm, hbm),
        scratch_shapes=[
            pltpu.VMEM((4, tokens, width), bf16),
            pltpu.VMEM((width, units), bf16),
            pltpu.VMEM((width, units), bf16),
            pltpu.VMEM((units, width), bf16),
            pltpu.VMEM((3, NX - 1, MSG, width), bf16),
            pltpu.VMEM((3, NX * MSG, width), bf16),
            pltpu.VMEM((3, 8, BLK, width), bf16),
            pltpu.VMEM((3, BLK, width), bf16),
            pltpu.VMEM((2, 8, BLK, width), bf16),
            pltpu.VMEM((2, 10, BLK, width), bf16),
            pltpu.VMEM((2, NX - 1, MSG, width), bf16),
            pltpu.VMEM((2, NX * MSG, width), bf16),
            pltpu.VMEM((2, tokens, width), bf16),
            dma((7,)),
            dma((3, NX - 1)),
            dma((3, NX - 1)),
            dma((3, 8, 2)),
            dma((3, 8)),
            dma((3,)),
            dma((2, 8)),
            dma((2, 10)),
            dma((2, NX - 1)),
            dma((2, NX - 1)),
            dma((2,)),
            dma((2,)),
        ],
        compiler_params=pltpu.CompilerParams(
            collective_id=0, has_side_effects=True, vmem_limit_bytes=67043328
        ),
        name="relay",
    )(
        pf, pb, pft, pbt, q, qt, fwd_weight[:, None],
        fwd_in[0], saved_in[0], weighted, grad_in[0], w_gate[0], w_up[0], w_down[0],
    )
    return out_f[None], out_b[None]


def solution(mesh):
    in_specs = (
        P("pp", "ep", None),
        P("pp", "ep", None),
        P("pp", "ep", None),
        P("pp", "ep", None),
        P("pp", "ep", None),
        P("pp", None, None),
        P("pp", None, "ep"),
        P("pp", None, "ep"),
        P("pp", "ep", None),
    )
    out_specs = (P("pp", "ep", None), P("pp", "ep", None))
    return jax.shard_map(
        per_device, mesh=mesh, in_specs=in_specs, out_specs=out_specs, check_vma=False
    )
```

time: 925 us -> 384 us (0.42)
  waiting for transfers between devices: 632 us -> 0 us
  Pallas kernels: 0 us -> 364 us
  local copies, waits for them, and re-layouts: 90.8 us -> 3.91 us
  other arithmetic: 65.5 us -> 4.79 us
  blocking collectives: 53.2 us -> 0 us
  starting transfers between devices: 45.1 us -> 0 us
  matrix products: 27 us -> 5.23 us
    ppermute x12 -> x0, waiting for transfers between devices: 515 us -> none  [the longest x10 504 us: swapped(): lax.ppermute(value, axis, [(i, i ^ 1 << distance) for i in range(lax.axis...]
    pallas_call x0 -> x1, Pallas kernels: none -> 364 us  [per_device(): pl.pallas_call(kernel, out_shape=(shape, shape), in_specs=[vmem] * 7 + [h...]
    all_to_all x4 -> x0, waiting for transfers between devices: 118 us -> none  [the longest x1 35.8 us: per_device(): lax.all_to_all(jnp.take(fwd_padded, fwd_index, axis=0), 'ep', split_axis=...]
    all_to_all x1 -> x0, blocking collectives: 53.2 us -> none  [per_device(): lax.all_to_all(jnp.take(saved_padded, bwd_index, axis=0), 'ep', split_axi...]
    select_n x14 -> x0, other arithmetic: 36.6 us -> none  [the longest x9 28.4 us: arrange(): jnp.where(own_bit == 0, jnp.stack([own_rows, peer_rows]), jnp.stack([peer...]
    all_to_all x4 -> x0, starting transfers between devices: 33.2 us -> none  [the longest x1 8.83 us: per_device(): lax.all_to_all(jnp.take(weighted_padded, bwd_index, axis=0), 'ep', split_...]
    select_n x8 -> x0, local copies, waits for them, and re-layouts: 28.3 us -> none  [the longest x6 28.1 us: arrange(): jnp.where(own_bit == 0, jnp.stack([own_rows, peer_rows]), jnp.stack([peer...]
    dot_general x7 -> x4, matrix products: 27 us -> 5.23 us  [the longest x2 4.18 us: routing_weight(): jnp.dot(tokens.astype(f32), router, precision=lax.Precision.HIGHEST)]
  transfers between devices with their start and end apart: 16 -> 0, of which waited for: 15 -> 0; matrix products, arithmetic and copies ran while one was open for 17% -> 0% of each run, Pallas kernels for 0% -> 0%
where the time goes in v1:
time: 384 us; the launch traced here: 378 us
  Pallas kernels  364 us (95%)
  matrix products  5.23 us (1%)
  other arithmetic  4.79 us (1%)
  local copies, waits for them, and re-layouts  3.91 us (1%)
    pallas_call x1, Pallas kernels, per_device(): pl.pallas_call(kernel, out_shape=(shape, shape), in_specs=[vmem] * 7 + [h...  364 us

profile of v1, /device:TPU:1, one launch (start us, length us, event | category | flops | bytes accessed | tf_op | source)
XLA Modules:
  0.0 378.2 jit_solution(17550408538517284157)
XLA Ops:
  0.6 0.0 copy-start
  0.6 0.0 copy-start.2
  0.7 2.1 fusion
  2.8 0.9 fusion.2
  3.7 0.7 fusion.20
  4.4 2.1 fusion.1
  6.5 0.0 copy-done.2
  6.5 0.2 fusion.3
  6.7 0.1 broadcast_add_fusion
  6.8 0.7 copy.11.fw
  7.5 0.7 fusion.5.q
  8.2 0.7 fusion.4.qt
  8.9 0.7 fusion.10
  9.6 0.8 fusion.6
  10.4 0.0 copy-done
  10.4 1.1 multiply_convert_fusion.wgt
  11.5 363.5 %relay.1 = (bf16[128,3584]{1,0:T(8,128)(2,1)}, bf16[128,3584]{1,0:T(8,128)(2,1)}) custom-call(bf16[192,128]{1,0:T(8,128)(2,1)} %get-tuple-element.8.pf, bf16[192,128]{1,0:T(8,128)(2,1)} %get-tuple-element.9.pb, bf16[128,192]{1,0:T(8,128)(2,1)} %get-tuple-element.6.pft, bf16[128,192]{1,0:T(8,128)(2,1)} %get-tuple-element.7.pbt, bf16[2,80,192]{2,1,0:T(8,128)(2,1)} %fusion.5.q, ...), custom_call_target="tpu_custom_call" | custom-call | tf_op jit(solution)/shard_map/relay/pallas_call | solution.py:433
  375.0 0.0 copy-start.1
  375.0 2.2 copy.14
  377.3 0.0 copy-done.1
  377.3 0.9 copy.15
  (5 shorter events, 0.1 us)
Async XLA Ops:
  0.6 9.7 %copy-start = (bf16[1,128,3584]{2,1,0:T(8,128)(2,1)S(1)}, bf16[1,128,3584]{2,1,0:T(8,128)(2,1)}, u32[]{:S(2)}) copy-start(bf16[1,128,3584]{2,1,0:T(8,128)(2,1)} %param.13) | copy-start | bytes 2752516
  0.6 5.8 %copy-start.2 = (s32[1,128,1]{1,2,0:T(1,128)S(1)}, s32[1,128,1]{1,2,0:T(1,128)}, u32[]{:S(2)}) copy-start(s32[1,128,1]{1,2,0:T(1,128)} %param.12) | copy-start | bytes 1540
  375.0 2.3 copy-start.1

commit v2 on v1

v2 whole, which is shorter than its diff:
```python
import functools

import jax
import jax.numpy as jnp
from jax import lax
from jax.experimental import pallas as pl
from jax.experimental.pallas import tpu as pltpu
from jax.sharding import PartitionSpec as P

route_scale = 2.5
MESH = pl.DeviceIdType.MESH
f32 = jnp.float32
bf16 = jnp.bfloat16

NX = 4
NZ = 8
SPAN = 4
CAP = 20
MSG = 48
BLK = NX * CAP
OWN = 7
FROM_LEFT, FROM_RIGHT, AWAY = 7, 8, 9
B_AT = 6
B_PREP = 3
LAG = 2
F_DONE = 12
COLS = 256
PARTS = 2


def nt(a, b):
    return lax.dot_general(a, b, (((1,), (1,)), ((), ())), preferred_element_type=f32)


def nn(a, b):
    return jnp.dot(a, b, preferred_element_type=f32)


def kernel(
    ids_f, ids_b, router, fwd, sav, grd, wg_h, wu_h, wd_h,
    out_f, out_b,
    pf, pb, pft, pbt, q, qt, fw,
    tok, wg, wu, wd, xs, xr, inb, away, part, back, ys, yr, sec,
    ld_sem, x_ss, x_rs, in_ss, in_rs, f_ss, o_ss, o_rs, y_ss, y_rs, pp_ss, pp_rs,
):
    width = tok.shape[2]
    chunks = width // COLS
    steps = chunks // PARTS
    span = width // PARTS
    both = range(PARTS)
    pp = lax.axis_index("pp")
    ep = lax.axis_index("ep")
    n_pp = lax.axis_size("pp")
    x = ep // NZ
    z = ep % NZ
    h = z // SPAN
    i = z % SPAN

    def at(xx, zz):
        return {"ep": (xx % NX) * NZ + (zz + NZ) % NZ}

    right = at(x, z + 1)
    left = at(x, z - 1)
    pp_up = {"pp": (pp + 1) % n_pp}
    pp_down = {"pp": (pp + n_pp - 1) % n_pp}

    loads = [
        pltpu.make_async_copy(src, dst, ld_sem.at[j])
        for j, (src, dst) in enumerate([
            (fwd, tok.at[0]), (sav, tok.at[1]), (grd, tok.at[3]),
            (wg_h, wg), (wu_h, wu), (wd_h, wd),
        ])
    ]
    for load in loads:
        load.start()

    barrier = pltpu.get_barrier_semaphore()
    friends = [at(x + 1, z), at(x + 2, z), at(x + 3, z), right, left, at(x, z + 2), at(x, z - 2), pp_up, pp_down]
    for friend in friends:
        pl.semaphore_signal(barrier, inc=1, device_id=friend, device_id_type=MESH)
    def remote(src, dst, ss, rs, dev):
        return pltpu.make_async_remote_copy(
            src_ref=src, dst_ref=dst, send_sem=ss, recv_sem=rs, device_id=dev, device_id_type=MESH
        )

    def cols(c):
        return pl.ds(pl.multiple_of(c * COLS, COLS), COLS)

    def cut(c):
        return pl.ds(c * span, span)

    def cut_cols(c, j):
        return pl.ds(pl.multiple_of(c * span + j * COLS, COLS), COLS)

    def rows48(k):
        return pl.ds(pl.multiple_of(k * MSG, 16), MSG)

    def iota(shape, axis):
        return lax.broadcasted_iota(jnp.int32, shape, axis).astype(f32)

    def ones(where):
        return jnp.where(where, 1.0, 0.0)

    def chosen(ids):
        count = ids.shape[1]
        same = iota((count, count), 0) == iota((count, count), 1)
        column = jnp.sum(jnp.where(same, ids[...].astype(f32), 0.0), axis=1, keepdims=True)
        return column == iota((count, 2 * NX), 1)

    def spots(ids, spread, gather):
        count = ids.shape[1]
        hot = ones(chosen(ids))
        earlier = ones(iota((count, count), 0) > iota((count, count), 1))
        before = nn(earlier.astype(bf16), hot.astype(bf16))
        expert = lax.broadcasted_iota(jnp.int32, (count, 2 * NX), 1)
        base = ((expert // 2) * MSG + (expert % 2) * CAP).astype(f32)
        place = jnp.sum(hot * (before + base), axis=1, keepdims=True)
        same = iota((count, count), 0) == iota((count, count), 1)
        place_row = jnp.sum(jnp.where(same, place, 0.0), axis=0, keepdims=True)
        gather[...] = ones(iota(gather.shape, 1) == place).astype(bf16)
        spread[...] = ones(iota(spread.shape, 0) == place_row).astype(bf16)

    def routing_weight(ids, t):
        count = ids.shape[1]
        logits = jnp.zeros((count, 2 * NX), f32)
        for c in range(width // 512):
            here = slice(c * 512, (c + 1) * 512)
            logits += lax.dot_general(
                tok[t, :, here].astype(f32), router[:, here], (((1,), (1,)), ((), ())),
                precision=lax.Precision.HIGHEST, preferred_element_type=f32,
            )
        logit = jnp.sum(jnp.where(chosen(ids), logits, 0.0), axis=1, keepdims=True)
        return route_scale * jax.nn.sigmoid(logit)

    def block_rows(shape, axis):
        row = iota(shape, axis)
        source = ones(row >= CAP) + ones(row >= 2 * CAP) + ones(row >= 3 * CAP)
        return row + (MSG - CAP) * source

    def block_picks():
        for half in range(2):
            shape = (BLK, NX * MSG)
            q[half] = ones(block_rows(shape, 0) + half * CAP == iota(shape, 1)).astype(bf16)
            shape = (NX * MSG, BLK)
            qt[half] = ones(block_rows(shape, 1) + half * CAP == iota(shape, 0)).astype(bf16)

    def x_copy(t, d, c):
        return remote(
            xs.at[t, d - 1, :, cut(c)], xr.at[t, rows48(x), cut(c)],
            x_ss.at[t, d - 1, c], x_rs.at[t, d - 1, c], at(x + d, z),
        )

    def x_arrival(t, d, c):
        return remote(
            xs.at[t, d - 1, :, cut(c)], xr.at[t, rows48((x + NX - d) % NX), cut(c)],
            x_ss.at[t, d - 1, c], x_rs.at[t, d - 1, c], at(x + d, z),
        )

    def x_send(t, p_ref):
        for c in both:
            for d in (2, 1, 3, 0):
                xd = (x + d) % NX

                @pl.loop(0, steps)
                def _(j, c=c, d=d, xd=xd):
                    picked = nn(p_ref[rows48(xd), :], tok[t, :, cut_cols(c, j)]).astype(bf16)
                    if d == 0:
                        xr[t, rows48(x), cut_cols(c, j)] = picked
                    else:
                        xs[t, d - 1, :, cut_cols(c, j)] = picked

                if d:
                    x_copy(t, d, c).start()

    def own_right(t, c):
        return remote(
            inb.at[t, OWN, :, cut(c)], inb.at[t, 0, :, cut(c)], in_ss.at[t, OWN, 0, c], in_rs.at[t, 0, c], right
        )

    def own_left(t, c):
        return remote(
            inb.at[t, OWN, :, cut(c)], inb.at[t, 6, :, cut(c)], in_ss.at[t, OWN, 1, c], in_rs.at[t, 6, c], left
        )

    def own_away(t, c):
        slot = jnp.where(i < 2, 6 - i, 3 - i)
        target = at(x, jnp.where(i < 2, z - 1 - i, z + 4 - i))
        return remote(away.at[t, :, cut(c)], inb.at[t, slot, :, cut(c)], f_ss.at[t, c], in_rs.at[t, slot, c], target)

    def pass_right(t, k, c):
        return remote(
            inb.at[t, k - 1, :, cut(c)], inb.at[t, k, :, cut(c)], in_ss.at[t, k - 1, 0, c], in_rs.at[t, k, c], right
        )

    def pass_left(t, k, c):
        return remote(
            inb.at[t, 7 - k, :, cut(c)], inb.at[t, 6 - k, :, cut(c)],
            in_ss.at[t, 7 - k, 1, c], in_rs.at[t, 6 - k, c], left,
        )

    def arrival(t, slot, c):
        here = inb.at[t, slot, :, cut(c)]
        return remote(here, here, in_ss.at[t, slot, 0, c], in_rs.at[t, slot, c], right)

    def has_l(k):
        return (k >= 1) & (k <= i + 2)

    def has_r(k):
        return (k >= 1) & (k <= 5 - i)

    def z_start(t):
        for c in both:
            for d in (1, 3, 2):
                x_arrival(t, d, c).wait_recv()

            @pl.loop(0, steps)
            def _(j, c=c):
                inb[t, OWN, :, cut_cols(c, j)] = nn(q[h], xr[t, :, cut_cols(c, j)]).astype(bf16)
                away[t, :, cut_cols(c, j)] = nn(q[1 - h], xr[t, :, cut_cols(c, j)]).astype(bf16)

            @pl.when(i < 3)
            def _(c=c):
                own_right(t, c).start()

            @pl.when(i > 0)
            def _(c=c):
                own_left(t, c).start()

            own_away(t, c).start()

    def z_step(t, k):
        for c in both:
            @pl.when(has_l(k))
            def _(c=c):
                arrival(t, k - 1, c).wait_recv()

                @pl.when(i < 3)
                def _():
                    pass_right(t, k, c).start()

            @pl.when(has_r(k))
            def _(c=c):
                arrival(t, 7 - k, c).wait_recv()

                @pl.when(i > 0)
                def _():
                    pass_left(t, k, c).start()

    def expert_forward(slot):
        gate = nn(inb[0, slot], wg[...])
        up = nn(inb[0, slot], wu[...])
        hidden = (gate * jax.nn.sigmoid(gate) * up).astype(bf16)

        @pl.loop(0, chunks)
        def _(c):
            part[0, slot, :, cols(c)] = nn(hidden, wd[:, cols(c)]).astype(bf16)

    def expert_backward(slot):
        gate = nn(inb[1, slot], wg[...])
        up = nn(inb[1, slot], wu[...])
        d_hidden = nt(inb[2, slot], wd[...])
        s = jax.nn.sigmoid(gate)
        d_gate = (d_hidden * up * s * (1.0 + gate * (1.0 - s))).astype(bf16)
        d_up = (d_hidden * gate * s).astype(bf16)

        @pl.loop(0, chunks)
        def _(c):
            part[1, slot, :, cols(c)] = (nt(d_gate, wg[cols(c), :]) + nt(d_up, wu[cols(c), :])).astype(bf16)

    def work(expert, k):
        @pl.loop(0, 2)
        def _(side):
            good = jnp.where(side == 0, has_l(k).astype(jnp.int32), ((k >= 0) & (k <= 5 - i)).astype(jnp.int32))

            @pl.when(good == 1)
            def _():
                expert(jnp.where(side == 0, k - 1, 7 - k))

    def back_left(o, k, c):
        slot = jnp.where(i == 0, AWAY, jnp.where(k >= 2, k - 2, FROM_RIGHT))
        return remote(
            part.at[o, k - 1, :, cut(c)], back.at[o, slot, :, cut(c)], o_ss.at[o, k - 1, c], o_rs.at[o, slot, c],
            at(x, jnp.where(i == 0, z - k, z - 1)),
        )

    def back_right(o, k, c):
        slot = jnp.where(i == 3, AWAY, jnp.where(k >= 2, 8 - k, FROM_LEFT))
        return remote(
            part.at[o, 7 - k, :, cut(c)], back.at[o, slot, :, cut(c)], o_ss.at[o, 7 - k, c], o_rs.at[o, slot, c],
            at(x, jnp.where(i == 3, z + k, z + 1)),
        )

    def returned(o, slot, c):
        here = back.at[o, slot, :, cut(c)]
        return remote(here, here, o_ss.at[o, 0, c], o_rs.at[o, slot, c], right)

    def add_in(o, slot, src, c):
        returned(o, src, c).wait_recv()

        @pl.loop(0, steps)
        def _(j):
            part[o, slot, :, cut_cols(c, j)] = (
                part[o, slot, :, cut_cols(c, j)].astype(f32) + back[o, src, :, cut_cols(c, j)].astype(f32)
            ).astype(bf16)

    def back_step(o, n):
        kl = n - LAG * (3 - i)
        kr = n - LAG * i
        for c in both:
            @pl.when(has_l(kl))
            def _(c=c):
                @pl.when(i < 3)
                def _():
                    add_in(o, kl - 1, kl - 1, c)

                back_left(o, kl, c).start()

            @pl.when(has_r(kr))
            def _(c=c):
                @pl.when(i > 0)
                def _():
                    add_in(o, 7 - kr, 7 - kr, c)

                back_right(o, kr, c).start()

    def y_copy(o, d, c):
        return remote(
            ys.at[o, d - 1, :, cut(c)], yr.at[o, rows48(x), cut(c)],
            y_ss.at[o, d - 1, c], y_rs.at[o, d - 1, c], at(x + d, z),
        )

    def y_arrival(o, d, c):
        return remote(
            ys.at[o, d - 1, :, cut(c)], yr.at[o, rows48((x + NX - d) % NX), cut(c)],
            y_ss.at[o, d - 1, c], y_rs.at[o, d - 1, c], at(x + d, z),
        )

    def y_send(o):
        for c in both:
            @pl.when(i > 0)
            def _(c=c):
                add_in(o, OWN, FROM_LEFT, c)

            @pl.when(i < 3)
            def _(c=c):
                add_in(o, OWN, FROM_RIGHT, c)

            returned(o, AWAY, c).wait_recv()
            for d in (2, 1, 3, 0):
                xd = (x + d) % NX

                @pl.loop(0, steps)
                def _(j, c=c, d=d, xd=xd):
                    picked = (
                        nn(qt[h, rows48(xd), :], part[o, OWN, :, cut_cols(c, j)])
                        + nn(qt[1 - h, rows48(xd), :], back[o, AWAY, :, cut_cols(c, j)])
                    ).astype(bf16)
                    if d == 0:
                        yr[o, rows48(x), cut_cols(c, j)] = picked
                    else:
                        ys[o, d - 1, :, cut_cols(c, j)] = picked

                if d:
                    y_copy(o, d, c).start()

    def pp_copy(o, c):
        if o == 0:
            return remote(sec.at[0, :, cut(c)], out_f.at[:, cut(c)], pp_ss.at[0, c], pp_rs.at[0, c], pp_up)
        return remote(sec.at[1, :, cut(c)], out_b.at[:, cut(c)], pp_ss.at[1, c], pp_rs.at[1, c], pp_down)

    def finish(o, pt_ref):
        for c in both:
            for d in (1, 3, 2):
                y_arrival(o, d, c).wait_recv()

            @pl.loop(0, steps)
            def _(j, c=c):
                here = cut_cols(c, j)
                expert_out = nn(pt_ref[...], yr[o, :, here]).astype(bf16).astype(f32)
                if o == 0:
                    sec[o, :, here] = (tok[0, :, here].astype(f32) + fw[...] * expert_out).astype(bf16)
                else:
                    sec[o, :, here] = (tok[3, :, here].astype(f32) + expert_out).astype(bf16)

            pp_copy(o, c).start()

    spots(ids_f, pf, pft)
    pl.semaphore_wait(barrier, len(friends))
    loads[0].wait()
    x_send(0, pf)
    spots(ids_b, pb, pbt)
    block_picks()
    loads[1].wait()
    x_send(1, pb)
    loads[2].wait()
    back_weight = routing_weight(ids_b, 1)
    for c in range(width // 512):
        here = slice(c * 512, (c + 1) * 512)
        tok[2, :, here] = (back_weight * tok[3, :, here].astype(f32)).astype(bf16)
    z_start(0)
    x_send(2, pb)
    fw[...] = routing_weight(ids_f, 0)
    for j in range(3, 6):
        loads[j].wait()

    last = B_AT + 5 + 3 * LAG

    @pl.loop(0, last + 1)
    def _(n):
        kb = n - B_AT

        @pl.when((n >= 1) & (n <= 5))
        def _():
            z_step(0, n)

        @pl.when(n == B_PREP)
        def _():
            z_start(1)
            z_start(2)

        @pl.when((kb >= 1) & (kb <= 5))
        def _():
            z_step(1, kb)
            z_step(2, kb)

        @pl.when(n <= 5)
        def _():
            work(expert_forward, n)

        @pl.when((kb >= 0) & (kb <= 5))
        def _():
            work(expert_backward, kb)

        back_step(0, n)
        back_step(1, kb)

        @pl.when(n == F_DONE)
        def _():
            y_send(0)

        @pl.when(n == F_DONE + 2)
        def _():
            finish(0, pft)

    y_send(1)
    finish(1, pbt)

    for c in both:
        for t in range(3):
            for d in (1, 2, 3):
                x_copy(t, d, c).wait_send()
            own_away(t, c).wait_send()

            @pl.when(i < 3)
            def _(t=t, c=c):
                own_right(t, c).wait_send()

            @pl.when(i > 0)
            def _(t=t, c=c):
                own_left(t, c).wait_send()

    @pl.loop(1, 6)
    def _(k):
        for c in both:
            for t in range(3):
                @pl.when(has_l(k) & (i < 3))
                def _(t=t, c=c):
                    pass_right(t, k, c).wait_send()

                @pl.when(has_r(k) & (i > 0))
                def _(t=t, c=c):
                    pass_left(t, k, c).wait_send()

            for o in range(2):
                @pl.when(has_l(k))
                def _(o=o, c=c):
                    back_left(o, k, c).wait_send()

                @pl.when(has_r(k))
                def _(o=o, c=c):
                    back_right(o, k, c).wait_send()

    for c in both:
        for o in range(2):
            for d in (1, 2, 3):
                y_copy(o, d, c).wait_send()
            pp_copy(o, c).wait_send()
            pp_copy(o, c).wait_recv()


def per_device(fwd_in, fwd_ids, saved_in, bwd_ids, grad_in, router, w_gate, w_up, w_down):
    experts = router.shape[-1]
    tokens, width = fwd_in.shape[1:]
    units = w_down.shape[1]
    assert lax.axis_size("ep") == NX * NZ and experts == 2 * NX and tokens == 128
    shape = jax.ShapeDtypeStruct((tokens, width), bf16)
    vmem = pl.BlockSpec(memory_space=pltpu.VMEM)
    hbm = pl.BlockSpec(memory_space=pl.ANY)
    dma = pltpu.SemaphoreType.DMA
    out_f, out_b = pl.pallas_call(
        kernel,
        out_shape=(shape, shape),
        in_specs=[vmem] * 3 + [hbm] * 6,
        out_specs=(hbm, hbm),
        scratch_shapes=[
            pltpu.VMEM((NX * MSG, tokens), bf16),
            pltpu.VMEM((NX * MSG, tokens), bf16),
            pltpu.VMEM((tokens, NX * MSG), bf16),
            pltpu.VMEM((tokens, NX * MSG), bf16),
            pltpu.VMEM((2, BLK, NX * MSG), bf16),
            pltpu.VMEM((2, NX * MSG, BLK), bf16),
            pltpu.VMEM((tokens, 1), f32),
            pltpu.VMEM((4, tokens, width), bf16),
            pltpu.VMEM((width, units), bf16),
            pltpu.VMEM((width, units), bf16),
            pltpu.VMEM((units, width), bf16),
            pltpu.VMEM((3, NX - 1, MSG, width), bf16),
            pltpu.VMEM((3, NX * MSG, width), bf16),
            pltpu.VMEM((3, 8, BLK, width), bf16),
            pltpu.VMEM((3, BLK, width), bf16),
            pltpu.VMEM((2, 8, BLK, width), bf16),
            pltpu.VMEM((2, 10, BLK, width), bf16),
            pltpu.VMEM((2, NX - 1, MSG, width), bf16),
            pltpu.VMEM((2, NX * MSG, width), bf16),
            pltpu.VMEM((2, tokens, width), bf16),
            dma((6,)),
            dma((3, NX - 1, PARTS)),
            dma((3, NX - 1, PARTS)),
            dma((3, 8, 2, PARTS)),
            dma((3, 8, PARTS)),
            dma((3, PARTS)),
            dma((2, 8, PARTS)),
            dma((2, 10, PARTS)),
            dma((2, NX - 1, PARTS)),
            dma((2, NX - 1, PARTS)),
            dma((2, PARTS)),
            dma((2, PARTS)),
        ],
        compiler_params=pltpu.CompilerParams(
            collective_id=0, has_side_effects=True, vmem_limit_bytes=67043328
        ),
        name="relay",
    )(
        fwd_ids[0].T, bwd_ids[0].T, jnp.swapaxes(router[0], 0, 1),
        fwd_in[0], saved_in[0], grad_in[0], w_gate[0], w_up[0], w_down[0],
    )
    return out_f[None], out_b[None]


def solution(mesh):
    in_specs = (
        P("pp", "ep", None),
        P("pp", "ep", None),
        P("pp", "ep", None),
        P("pp", "ep", None),
        P("pp", "ep", None),
        P("pp", None, None),
        P("pp", None, "ep"),
        P("pp", None, "ep"),
        P("pp", "ep", None),
    )
    out_specs = (P("pp", "ep", None), P("pp", "ep", None))
    return jax.shard_map(
        per_device, mesh=mesh, in_specs=in_specs, out_specs=out_specs, check_vma=False
    )
```

time: 384 us -> 362 us (0.943); the launches traced: 378 us -> 360 us
  Pallas kernels: 364 us -> 356 us
  matrix products: 5.23 us -> 0 us
  other arithmetic: 4.79 us -> 0 us
    pallas_call x1, Pallas kernels: 364 us -> 356 us  [per_device(): pl.pallas_call(kernel, out_shape=(shape, shape), in_specs=[vmem] * 3 + [h...]
    dot_general x4 -> x0, matrix products: 5.23 us -> none  [the longest x2 4.18 us: routing_weight(): jnp.dot(tokens.astype(f32), router, precision=lax.Precision.HIGHEST)]
    convert_element_type x5 -> x0, other arithmetic: 3.97 us -> none  [the longest x1 1.14 us: per_device(): weighted = (bwd_weight[:, None] * grad_in[0].astype(f32)).astype(bf16)]
where the time goes in v2:
time: 362 us; the launch traced here: 360 us
  Pallas kernels  356 us (98%)
    pallas_call x1, Pallas kernels, per_device(): pl.pallas_call(kernel, out_shape=(shape, shape), in_specs=[vmem] * 3 + [h...  356 us

profile of v2, /device:TPU:1, one launch (start us, length us, event | category | flops | bytes accessed | tf_op | source)
XLA Modules:
  0.0 360.3 jit_solution(7323911107532414904)
XLA Ops:
  0.6 356.4 %relay.1 = (bf16[128,3584]{1,0:T(8,128)(2,1)}, bf16[128,3584]{1,0:T(8,128)(2,1)}) custom-call(s32[1,128]{1,0:T(1,128)} %bitcast.22, s32[1,128]{1,0:T(1,128)} %bitcast.23, f32[8,3584]{1,0:T(8,128)} %bitcast.21, bf16[128,3584]{1,0:T(8,128)(2,1)} %bitcast.16, bf16[128,3584]{1,0:T(8,128)(2,1)} %bitcast.17, bf16[128,3584]{1,0:T(8,128)(2,1)} %bitcast.18, ...), custom_call_target="tpu_custom_call" | custom-call | tf_op jit(solution)/shard_map/relay/pallas_call | solution.py:500
  357.1 0.0 copy-start
  357.1 2.2 copy.13
  359.3 0.0 copy-done
  359.3 0.9 copy.14
Async XLA Ops:
  357.1 2.3 copy-start

commit v3 on v2

--- a/solution.py
+++ b/solution.py
@@ -24,8 +24,8 @@
 B_PREP = 3
 LAG = 2
 F_DONE = 12
-COLS = 256
-PARTS = 2
+COLS = 896
+PARTS = 4
 
 
 def nt(a, b):

time: 362 us -> 348 us (0.961)
  Pallas kernels: 356 us -> 344 us
    pallas_call x1, Pallas kernels: 356 us -> 344 us  [per_device(): pl.pallas_call(kernel, out_shape=(shape, shape), in_specs=[vmem] * 3 + [h...]
where the time goes in v3:
time: 348 us
  Pallas kernels  344 us (99%)
    pallas_call x1, Pallas kernels, per_device(): pl.pallas_call(kernel, out_shape=(shape, shape), in_specs=[vmem] * 3 + [h...  344 us

profile of v3, /device:TPU:1, one launch (start us, length us, event | category | flops | bytes accessed | tf_op | source)
XLA Modules:
  0.0 347.6 jit_solution(4960578272704005260)
XLA Ops:
  0.6 343.8 %relay.1 = (bf16[128,3584]{1,0:T(8,128)(2,1)}, bf16[128,3584]{1,0:T(8,128)(2,1)}) custom-call(s32[1,128]{1,0:T(1,128)} %bitcast.22, s32[1,128]{1,0:T(1,128)} %bitcast.23, f32[8,3584]{1,0:T(8,128)} %bitcast.21, bf16[128,3584]{1,0:T(8,128)(2,1)} %bitcast.16, bf16[128,3584]{1,0:T(8,128)(2,1)} %bitcast.17, bf16[128,3584]{1,0:T(8,128)(2,1)} %bitcast.18, ...), custom_call_target="tpu_custom_call" | custom-call | tf_op jit(solution)/shard_map/relay/pallas_call | solution.py:500
  344.4 0.0 copy-start
  344.4 2.2 copy.13
  346.7 0.0 copy-done
  346.7 0.9 copy.14
Async XLA Ops:
  344.4 2.3 copy-start
